TPU v7x, 32 devices: a whole 2x2x4 slice. The times are simulated.
32 devices in a mesh: groups: 2 (over y), rows: 4 (over x, core), seq: 4 (over z).
Axes of the slice: x: 2, y: 2, z: 4, core: 2. Of those that a mesh axis runs over, the one named last changes fastest.
Arguments:
- activations: bfloat16 [2, 8, 512, 4096], P(None, ('groups', 'rows'), 'seq'), parts along dimension 1, may hold values from -6 to 6
- out_grads: bfloat16 [2, 8, 512, 4096], P(None, ('groups', 'rows'), 'seq'), parts along dimension 1, may hold values from -6 to 6
- lengths: int32 [8], P(('groups', 'rows')), parts along dimension 0, may hold values from 64 to 512
- proj_in: bfloat16 [2, 4096, 64], replicated, may hold values from -0.09375 to 0.09375
- proj_out: bfloat16 [2, 4096, 64], replicated, may hold values from -0.09375 to 0.09375
- basis_in: float32 [2, 64, 64], replicated, may hold values from -0.75 to 0.75
- basis_out: float32 [2, 64, 64], replicated, may hold values from -0.75 to 0.75
- eigen: float32 [2, 64, 64], replicated, may hold values from 10 to 1000
- store: bfloat16 [1024, 8192], P(('groups', 'rows', 'seq')), parts along dimension 0, may hold values from -0.0625 to 0.0625
- candidates: int32 [8, 64], P('groups'), parts along dimension 0, may hold values from 0 to 511
Outputs:
- scores: float32 [1024, 4], P(('groups', 'rows', 'seq')), parts along dimension 0
- picked: float32 [8, 64], P('groups'), parts along dimension 0
There are 2 independent parts, one for each index of `groups`. A program takes and returns all parts, laid end to end along the dimension named above; an argument that names none is the same for every part. Nothing has to cross between parts.
All inputs are finite; a program needn't handle non-finite values.
Results may differ from a plain program's by a relative error of at most 0.005.
Values may be sent and summed in bfloat16 or wider, within the bound.
A program may use at most 64 MiB of HBM per device.

v0:
```python
import jax
import jax.numpy as jnp
from jax import lax
from jax.sharding import PartitionSpec as P

damping = 1.0


def body(
    activations,
    out_grads,
    lengths,
    proj_in,
    proj_out,
    basis_in,
    basis_out,
    eigen,
    store,
    candidates,
):
    nl, bdev, tok, width = activations.shape
    high = lax.Precision.HIGHEST
    offset = lax.axis_index("seq") * tok
    positions = offset + jnp.arange(tok, dtype=jnp.int32)
    mask = (positions[None, :] < lengths[:, None]).astype(jnp.bfloat16)
    pa = jnp.einsum("lbtd,ldr->lbtr", activations, proj_in, preferred_element_type=jnp.float32)
    pg = jnp.einsum("lbtd,ldr->lbtr", out_grads, proj_out, preferred_element_type=jnp.float32)
    pa = pa.astype(jnp.bfloat16) * mask[None, :, :, None]
    pg = pg.astype(jnp.bfloat16) * mask[None, :, :, None]
    local = jnp.einsum("lbto,lbti->lboi", pg, pa, preferred_element_type=jnp.float32)
    total = lax.psum(local, "seq")
    rot = jnp.einsum("loj,lboi,lik->lbjk", basis_out, total, basis_in, precision=high)
    pre = rot / (eigen[:, None] + damping)
    back = jnp.einsum("loj,lbjk,lik->lboi", basis_out, pre, basis_in, precision=high)
    test = jnp.transpose(back, (1, 0, 2, 3)).reshape(bdev, -1).astype(jnp.bfloat16)
    scores = jnp.dot(
        store,
        lax.all_gather(test, "rows", axis=0, tiled=True).T,
        preferred_element_type=jnp.float32,
    )
    rdev = store.shape[0]
    row_start = (lax.axis_index("rows") * lax.axis_size("seq") + lax.axis_index("seq")) * rdev
    local_index = candidates - row_start
    onehot = (local_index[:, :, None] == jnp.arange(rdev, dtype=jnp.int32)[None, None, :]).astype(
        jnp.float32
    )
    picked_local = jnp.einsum("bkr,rb->bk", onehot, scores, precision=high)
    picked = lax.psum(picked_local, ("rows", "seq"))
    return (scores, picked)


def solution(mesh):
    placed = (
        P(None, ("groups", "rows"), "seq", None),
        P(None, ("groups", "rows"), "seq", None),
        P(("groups", "rows")),
        P(),
        P(),
        P(),
        P(),
        P(),
        P(("groups", "rows", "seq"), None),
        P("groups", None),
    )
    return jax.shard_map(
        body,
        mesh=mesh,
        in_specs=placed,
        out_specs=(P(("groups", "rows", "seq"), None), P("groups", None)),
        check_vma=False,
    )
```

profile of v0, /device:TPU:0, one launch (start us, length us, event | category | flops | bytes accessed | tf_op | source)
XLA Modules:
  0.0 67.5 jit_solution(14491491141330753)
XLA Ops:
  0.6 0.0 copy-start
  0.6 0.0 copy-start.1
  1.5 0.8 %copy-done = bf16[2,1,128,4096]{3,2,1,0:T(8,128)(2,1)S(1)} copy-done((bf16[2,1,128,4096]{3,2,1,0:T(8,128)(2,1)S(1)}, bf16[2,1,128,4096]{3,2,1,0:T(8,128)(2,1)}, u32[]{:S(2)}) %copy-start) | copy-done | bytes 2097176
  2.2 2.1 %fusion.16 = bf16[2,128,64]{1,2,0:T(8,128)(2,1)S(1)} fusion(bf16[2,4096,64]{1,2,0:T(8,128)(2,1)} %param.14, bf16[2,1,128,4096]{3,2,1,0:T(8,128)(2,1)S(1)} %copy-done, bf16[128]{0:T(256)(128)(2,1)S(1)} %compare_convert_fusion), kind=kOutput, calls=%fused_computation.10 | convolution fusion | flops 134250496 | bytes 3178752 | tf_op jit(solution)/shard_map/lbtd,ldr->lbtr/dot_general | solution.py:27
  4.3 0.0 copy-done.1
  4.3 0.0 copy-start.2
  4.3 0.0 copy-start.3
  4.3 0.0 copy-start.4
  4.4 0.0 copy-start.5
  4.4 2.7 %fusion.14 = f32[2,64,64]{2,1,0:T(8,128)S(1)} fusion(bf16[2,128,64]{1,2,0:T(8,128)(2,1)S(1)} %fusion.16, bf16[2,4096,64]{1,2,0:T(8,128)(2,1)S(1)} %copy-done.1, bf16[2,1,128,4096]{3,2,1,0:T(8,128)(2,1)} %param.10, bf16[128]{0:T(256)(128)(2,1)S(1)} %compare_convert_fusion), kind=kOutput, calls=%fused_computation.9 | convolution fusion | flops 136347648 | bytes 3211520 | tf_op jit(solution)/shard_map/lbto,lbti->lboi/dot_general | solution.py:30
  7.0 21.5 %psum.14 = f32[2,64,64]{2,1,0:T(8,128)S(1)} all-reduce(f32[2,64,64]{2,1,0:T(8,128)S(1)} %fusion.14), channel_id=1, replica_groups=mesh['groups'=2,'rows'=4,'seq'=4] {'seq'}, use_global_device_ids=true, to_apply=%region_0.0 | all-reduce | flops 8192 | bytes 65536 | tf_op jit(solution)/shard_map/psum | solution.py:31
  28.6 0.0 copy-done.2
  28.6 0.3 fusion.25
  28.9 0.0 copy-done.3
  28.9 0.0 copy-done.4
  28.9 0.2 convolution_divide_fusion
  29.1 0.2 fusion.26
  29.3 0.2 convolution_convert_fusion
  29.5 0.1 reshape.69
  29.6 5.4 %all-gather = bf16[4,1,8192]{2,1,0:T(2,128)(2,1)S(1)} all-gather(bf16[1,1,8192]{2,1,0:T(2,128)(2,1)S(1)} %reshape.69), channel_id=1, replica_groups=mesh['groups'=2,'rows'=4,'seq'=4] {'rows'}, dimensions={0}, use_global_device_ids=true | all-gather | bytes 81920 | tf_op jit(solution)/shard_map/all_gather | solution.py:38
  35.0 1.3 %fusion.20 = f32[4,32]{1,0:T(4,128)S(1)} fusion(bf16[32,8192]{1,0:T(8,128)(2,1)} %param.18, bf16[4,1,8192]{2,1,0:T(2,128)(2,1)S(1)} %all-gather), kind=kOutput, calls=%fused_computation.13 | convolution fusion | flops 2097152 | bytes 590336 | tf_op jit(solution)/shard_map/dot_general | solution.py:36
  36.3 0.0 copy-start.6
  36.3 0.0 copy-done.5
  36.3 0.3 fusion.19
  36.6 30.9 %psum.15 = f32[4,64]{1,0:T(4,128)} all-reduce(f32[4,64]{1,0:T(4,128)S(1)} %bitcast.41), channel_id=1, replica_groups=mesh['groups'=2,'rows'=4,'seq'=4] {'rows','seq'}, use_global_device_ids=true, to_apply=%region_1.0 | all-reduce | flops 256 | bytes 2048 | tf_op jit(solution)/shard_map/psum | solution.py:48
  67.5 0.0 copy-done.6
  (2 shorter events, 0.0 us)
Async XLA Ops:
  0.6 1.6 %copy-start = (bf16[2,1,128,4096]{3,2,1,0:T(8,128)(2,1)S(1)}, bf16[2,1,128,4096]{3,2,1,0:T(8,128)(2,1)}, u32[]{:S(2)}) copy-start(bf16[2,1,128,4096]{3,2,1,0:T(8,128)(2,1)} %param.11) | copy-start | bytes 6291460
  0.6 3.7 %copy-start.1 = (bf16[2,4096,64]{1,2,0:T(8,128)(2,1)S(1)}, bf16[2,4096,64]{1,2,0:T(8,128)(2,1)}, u32[]{:S(2)}) copy-start(bf16[2,4096,64]{1,2,0:T(8,128)(2,1)} %param.13) | copy-start | bytes 3145732
  4.3 24.2 %copy-start.2 = (f32[2,64,64]{2,1,0:T(8,128)S(1)}, f32[2,64,64]{2,1,0:T(8,128)}, u32[]{:S(2)}) copy-start(f32[2,64,64]{2,1,0:T(8,128)} %param.16) | copy-start | bytes 98308
  4.3 24.5 %copy-start.3 = (f32[2,64,64]{2,1,0:T(8,128)S(1)}, f32[2,64,64]{2,1,0:T(8,128)}, u32[]{:S(2)}) copy-start(f32[2,64,64]{2,1,0:T(8,128)} %param.15) | copy-start | bytes 98308
  4.3 24.5 %copy-start.4 = (f32[2,64,64]{2,1,0:T(8,128)S(1)}, f32[2,64,64]{2,1,0:T(8,128)}, u32[]{:S(2)}) copy-start(f32[2,64,64]{2,1,0:T(8,128)} %param.17) | copy-start | bytes 98308
  4.4 32.0 %copy-start.5 = (s32[4,64]{1,0:T(4,128)S(1)}, s32[4,64]{1,0:T(4,128)}, u32[]{:S(2)}) copy-start(s32[4,64]{1,0:T(4,128)} %param.19) | copy-start | bytes 3076
  36.3 31.2 %copy-start.6 = (f32[4,32]{1,0:T(4,128)}, f32[4,32]{1,0:T(4,128)S(1)}, u32[]{:S(2)}) copy-start(f32[4,32]{1,0:T(4,128)S(1)} %fusion.20) | copy-start | bytes 1540
where the time goes:
time: 67.8 us; the launch traced here: 67.5 us
  blocking collectives  57.9 us (85%)
  matrix products  7.18 us (11%)
  between operations  1.57 us (2%)
  local copies, waits for them, and re-layouts  0.91 us (1%)
    psum x1, blocking collectives, body(): picked = lax.psum(picked_local, ('rows', 'seq'))  30.9 us
    psum x1, blocking collectives, body(): total = lax.psum(local, 'seq')  21.5 us
    all_gather x1, blocking collectives, body(): lax.all_gather(test, 'rows', axis=0, tiled=True)  5.43 us
    dot_general x1, matrix products, body(): jnp.einsum('lbto,lbti->lboi', pg, pa, preferred_element_type=jnp.float32)  2.65 us
    dot_general x1, matrix products, body(): jnp.einsum('lbtd,ldr->lbtr', out_grads, proj_out, preferred_element_type=...  2.06 us

commit v1 on v0

v1 whole, which is shorter than its diff:
```python
import functools

import jax
import jax.numpy as jnp
from jax import lax
from jax.experimental import pallas as pl
from jax.experimental.pallas import tpu as pltpu
from jax.sharding import PartitionSpec as P

damping = 1.0
MESH = pl.DeviceIdType.MESH
F32 = jnp.float32
BF16 = jnp.bfloat16
NN = (((1,), (0,)), ((), ()))
NT = (((1,), (1,)), ((), ()))


def mm(a, b, dims=NN):
    return lax.dot_general(a, b, dims, preferred_element_type=F32)


def split(x):
    hi = x.astype(BF16)
    return hi, (x - hi.astype(F32)).astype(BF16)


def mm3(a, b, dims=NN):
    return mm(a[0], b[0], dims) + (mm(a[0], b[1], dims) + mm(a[1], b[0], dims))


def each(count, step):
    if count <= 16:
        for i in range(count):
            step(i)
    else:
        lax.fori_loop(0, count, lambda i, c: (step(i), c)[1], 0)


def kernel(
    nr, ns, lengths,
    acts_hbm, grads_hbm, pin_hbm, pout_hbm, bin_hbm, bout_hbm, eig_hbm, store_hbm, cand_hbm,
    scores_ref, picked_ref,
    acts, grads, pin, pout, bin_, bout, eig, store, cand,
    gsend, grecv, tsend, trecv, psend, precv,
    load_sem, small_sem, gs_sem, gr_sem, ts_sem, tr_sem, ps_sem, pr_sem,
):
    nl, tok, width = acts.shape
    rank = pin.shape[1]
    rdev = store.shape[0]
    half = rank // 2
    n = nr * ns
    row, seq = lax.axis_index("rows"), lax.axis_index("seq")
    me = row * ns + seq

    loads = []
    for l in range(nl):
        loads.append([
            pltpu.make_async_copy(src, dst, load_sem.at[l, i])
            for i, (src, dst) in enumerate((
                (pin_hbm.at[l], pin.at[l]),
                (acts_hbm.at[l, 0], acts.at[l]),
                (pout_hbm.at[l], pout.at[l]),
                (grads_hbm.at[l, 0], grads.at[l]),
            ))
        ])
    small = [
        pltpu.make_async_copy(src, dst, small_sem.at[i])
        for i, (src, dst) in enumerate((
            (bin_hbm, bin_), (bout_hbm, bout), (eig_hbm, eig), (cand_hbm, cand), (store_hbm, store),
        ))
    ]
    for c in small[:4]:
        c.start()
    for group in loads:
        for c in group:
            c.start()
    small[4].start()

    barrier = pltpu.get_barrier_semaphore()

    def peer(e):
        to = lax.rem(me + e + 1, n)
        return {"rows": to // ns, "seq": lax.rem(to, ns)}

    each(n - 1, lambda e: pl.semaphore_signal(
        barrier, inc=1, device_id=peer(e), device_id_type=MESH))

    for c in small[:3]:
        c.wait()
    i0 = lax.broadcasted_iota(jnp.int32, (rank, rank), 0)
    i1 = lax.broadcasted_iota(jnp.int32, (rank, rank), 1)
    order = (i1 == jnp.where(i0 < half, 2 * i0, 2 * (i0 - half) + 1)).astype(BF16)
    bi, bi2, bot, beo = [], [], [], []
    for l in range(nl):
        b = split(bin_[l])
        bi.append(b)
        bi2.append(tuple(jnp.concatenate([x, x], axis=0) for x in b))
        bot.append(split(jnp.transpose(bout[l])))
        beo.append(tuple(mm(order, x).astype(BF16) for x in split(bout[l])))

    pos = seq * tok + lax.broadcasted_iota(jnp.int32, (tok, rank), 0)
    keep = pos < lengths[0]

    def gcopy(l, d):
        return pltpu.make_async_remote_copy(
            src_ref=gsend.at[l], dst_ref=grecv.at[l, d],
            send_sem=gs_sem.at[l, d], recv_sem=gr_sem.at[l, d],
            device_id={"seq": lax.rem(seq + d + 1, ns)}, device_id_type=MESH)

    own = []
    for l in range(nl):
        loads[l][0].wait()
        loads[l][1].wait()
        pa = mm(acts[l], pin[l], NT).astype(BF16)
        pa = jnp.where(keep, pa.astype(F32), 0.0).astype(BF16)
        loads[l][2].wait()
        loads[l][3].wait()
        pgt = mm(pout[l], grads[l], NT).astype(BF16)
        g = mm(pgt, pa)
        own.append(g)
        gsend[l] = g.astype(BF16)
        if l == 0:
            pl.semaphore_wait(barrier, n - 1)
        each(ns - 1, lambda d: gcopy(l, d).start())

    tests = []
    for l in range(nl):
        total = own[l]
        for d in range(ns - 1):
            gcopy(l, d).wait_recv()
            total = total + grecv[l, d].astype(F32)
        y = mm3(split(total), bi[l])
        rot = mm3(bot[l], split(y))
        pre = rot / (eig[l] + damping)
        x2 = mm3(split(pre), bi2[l], NT)
        z = mm3(beo[l], split(x2))
        lane = lax.broadcasted_iota(jnp.int32, (half, 2 * rank), 1)
        t = jnp.where(lane < rank, z[:half], z[half:]).astype(BF16)
        tsend[pl.ds(l * half, half), :] = t
        tests.append(t)

    def tcopy(d):
        return pltpu.make_async_remote_copy(
            src_ref=tsend, dst_ref=trecv.at[d],
            send_sem=ts_sem.at[d], recv_sem=tr_sem.at[d],
            device_id={"rows": lax.rem(row + d + 1, nr)}, device_id_type=MESH)

    each(nr - 1, lambda d: tcopy(d).start())

    for c in small[3:]:
        c.wait()
    lanes = 2 * rank
    chunks = nl * half
    eye = lax.broadcasted_iota(jnp.int32, (rdev, rdev), 0) == lax.broadcasted_iota(
        jnp.int32, (rdev, rdev), 1)
    rows_k = me * rdev + lax.broadcasted_iota(jnp.int32, (rdev, cand.shape[1]), 0)

    def score(t, b):
        acc = [jnp.zeros((rdev, lanes), F32) for _ in range(2)]
        for c in range(chunks):
            s = store[:, c * lanes:(c + 1) * lanes].astype(F32)
            acc[c % 2] = acc[c % 2] + s * t[c:c + 1, :]
        col = jnp.sum(acc[0] + acc[1], axis=1, keepdims=True)
        scores_ref[pl.ds(b, 1), :] = jnp.sum(jnp.where(eye, col, 0.0), axis=0, keepdims=True)
        hit = cand[pl.ds(b, 1), :] == rows_k
        psend[pl.ds(b, 1), :] = jnp.sum(jnp.where(hit, col, 0.0), axis=0, keepdims=True)

    score(tsend[...].astype(F32), row)

    def other(d):
        tcopy(d).wait_recv()
        score(trecv[d].astype(F32), lax.rem(row + nr - d - 1, nr))

    each(nr - 1, other)

    def pcopy(e):
        return pltpu.make_async_remote_copy(
            src_ref=psend, dst_ref=precv.at[e],
            send_sem=ps_sem.at[e], recv_sem=pr_sem.at[e],
            device_id=peer(e), device_id_type=MESH)

    each(n - 1, lambda e: pcopy(e).start())
    picked_ref[...] = psend[...]

    for l in range(nl):
        each(ns - 1, lambda d: gcopy(l, d).wait_send())
    each(nr - 1, lambda d: tcopy(d).wait_send())

    def add(e):
        pcopy(e).wait_recv()
        picked_ref[...] += precv[e]

    each(n - 1, add)
    each(n - 1, lambda e: pcopy(e).wait_send())


def body(nr, ns, activations, out_grads, lengths, proj_in, proj_out,
         basis_in, basis_out, eigen, store, candidates):
    nl, _, tok, width = activations.shape
    rank = proj_in.shape[2]
    rdev, flat = store.shape
    batch, topk = candidates.shape
    n = nr * ns
    dma = pltpu.SemaphoreType.DMA
    vm = pltpu.VMEM
    hbm = pl.BlockSpec(memory_space=pl.ANY)
    scores, picked = pl.pallas_call(
        functools.partial(kernel, nr, ns),
        out_shape=(
            jax.ShapeDtypeStruct((batch, rdev), F32),
            jax.ShapeDtypeStruct((batch, topk), F32),
        ),
        in_specs=[pl.BlockSpec(memory_space=pltpu.SMEM)] + [hbm] * 9,
        out_specs=(pl.BlockSpec(memory_space=pltpu.VMEM),) * 2,
        scratch_shapes=[
            vm((nl, tok, width), BF16), vm((nl, tok, width), BF16),
            vm((nl, rank, width), BF16), vm((nl, rank, width), BF16),
            vm((nl, rank, rank), F32), vm((nl, rank, rank), F32), vm((nl, rank, rank), F32),
            vm((rdev, flat), BF16), vm((batch, topk), jnp.int32),
            vm((nl, rank, rank), BF16), vm((nl, ns - 1, rank, rank), BF16),
            vm((nl * rank // 2, 2 * rank), BF16), vm((nr - 1, nl * rank // 2, 2 * rank), BF16),
            vm((batch, topk), F32), vm((n - 1, batch, topk), F32),
            dma((nl, 4)), dma((5,)),
            dma((nl, ns - 1)), dma((nl, ns - 1)),
            dma((nr - 1,)), dma((nr - 1,)),
            dma((n - 1,)), dma((n - 1,)),
        ],
        compiler_params=pltpu.CompilerParams(
            collective_id=0, has_side_effects=True, vmem_limit_bytes=32 * 2**20),
    )(
        lengths, activations, out_grads,
        jnp.swapaxes(proj_in, 1, 2), jnp.swapaxes(proj_out, 1, 2),
        basis_in, basis_out, eigen, store, candidates,
    )
    return scores.T, picked


def solution(mesh):
    placed = (
        P(None, ("groups", "rows"), "seq", None),
        P(None, ("groups", "rows"), "seq", None),
        P(("groups", "rows")),
        P(),
        P(),
        P(),
        P(),
        P(),
        P(("groups", "rows", "seq"), None),
        P("groups", None),
    )
    return jax.shard_map(
        functools.partial(body, mesh.shape["rows"], mesh.shape["seq"]),
        mesh=mesh,
        in_specs=placed,
        out_specs=(P(("groups", "rows", "seq"), None), P("groups", None)),
        check_vma=False,
    )
```

time: 67.8 us -> 33.4 us (0.49)
  blocking collectives: 57.9 us -> 0 us
  Pallas kernels: 0 us -> 20.6 us
  local copies, waits for them, and re-layouts: 0.91 us -> 11 us
  matrix products: 7.18 us -> 0 us
    psum x2 -> x0, blocking collectives: 52.4 us -> none  [the longest x1 30.9 us: body(): picked = lax.psum(picked_local, ('rows', 'seq'))]
    pallas_call x0 -> x1, Pallas kernels: none -> 20.6 us  [body(): pl.pallas_call(functools.partial(kernel, nr, ns), out_shape=(jax.ShapeDty...]
    unnamed x15 -> x20, local copies, waits for them, and re-layouts: 0.91 us -> 11 us
    dot_general x8 -> x0, matrix products: 7.18 us -> none  [the longest x1 2.65 us: body(): jnp.einsum('lbto,lbti->lboi', pg, pa, preferred_element_type=jnp.float32)]
    all_gather x1 -> x0, blocking collectives: 5.43 us -> none  [body(): lax.all_gather(test, 'rows', axis=0, tiled=True)]
where the time goes in v1:
time: 33.4 us; the launch traced here: 32.9 us
  Pallas kernels  20.6 us (62%)
  local copies, waits for them, and re-layouts  11 us (33%)
  between operations  1.3 us (4%)
    pallas_call x1, Pallas kernels, body(): pl.pallas_call(functools.partial(kernel, nr, ns), out_shape=(jax.ShapeDty...  20.6 us
    unnamed x20, local copies, waits for them, and re-layouts  11 us

profile of v1, /device:TPU:0, one launch (start us, length us, event | category | flops | bytes accessed | tf_op | source)
XLA Modules:
  0.0 32.9 jit_solution(14889424237195149946)
XLA Ops:
  1.3 0.0 copy-start
  1.3 1.6 %copy-done = bf16[2,1,128,4096]{3,2,1,0:T(8,128)(2,1)S(1)} copy-done((bf16[2,1,128,4096]{3,2,1,0:T(8,128)(2,1)S(1)}, bf16[2,1,128,4096]{3,2,1,0:T(8,128)(2,1)}, u32[]{:S(2)}) %copy-start) | copy-done | bytes 2097176
  2.9 0.0 copy-start.1
  2.9 1.6 %copy-done.1 = bf16[2,1,128,4096]{3,2,1,0:T(8,128)(2,1)S(1)} copy-done((bf16[2,1,128,4096]{3,2,1,0:T(8,128)(2,1)S(1)}, bf16[2,1,128,4096]{3,2,1,0:T(8,128)(2,1)}, u32[]{:S(2)}) %copy-start.1) | copy-done | bytes 2097176
  4.5 0.0 copy-start.2
  4.5 1.2 %copy-done.2 = bf16[2,4096,64]{1,2,0:T(8,128)(2,1)S(1)} copy-done((bf16[2,4096,64]{1,2,0:T(8,128)(2,1)S(1)}, bf16[2,4096,64]{1,2,0:T(8,128)(2,1)}, u32[]{:S(2)}) %copy-start.2) | copy-done | bytes 1048600
  5.7 0.0 copy-start.3
  5.7 1.2 %copy-done.3 = bf16[2,4096,64]{1,2,0:T(8,128)(2,1)S(1)} copy-done((bf16[2,4096,64]{1,2,0:T(8,128)(2,1)S(1)}, bf16[2,4096,64]{1,2,0:T(8,128)(2,1)}, u32[]{:S(2)}) %copy-start.3) | copy-done | bytes 1048600
  6.9 0.0 copy-start.4
  6.9 1.0 %copy-done.4 = bf16[32,8192]{1,0:T(8,128)(2,1)S(1)} copy-done((bf16[32,8192]{1,0:T(8,128)(2,1)S(1)}, bf16[32,8192]{1,0:T(8,128)(2,1)}, u32[]{:S(2)}) %copy-start.4) | copy-done | bytes 524312
  8.0 0.0 copy-start.5
  8.0 0.8 %copy-done.5 = f32[2,64,64]{2,1,0:T(8,128)S(1)} copy-done((f32[2,64,64]{2,1,0:T(8,128)S(1)}, f32[2,64,64]{2,1,0:T(8,128)}, u32[]{:S(2)}) %copy-start.5) | copy-done | bytes 32792
  8.8 0.0 copy-start.6
  8.8 0.8 %copy-done.6 = f32[2,64,64]{2,1,0:T(8,128)S(1)} copy-done((f32[2,64,64]{2,1,0:T(8,128)S(1)}, f32[2,64,64]{2,1,0:T(8,128)}, u32[]{:S(2)}) %copy-start.6) | copy-done | bytes 32792
  9.6 0.0 copy-start.7
  9.6 0.8 %copy-done.7 = f32[2,64,64]{2,1,0:T(8,128)S(1)} copy-done((f32[2,64,64]{2,1,0:T(8,128)S(1)}, f32[2,64,64]{2,1,0:T(8,128)}, u32[]{:S(2)}) %copy-start.7) | copy-done | bytes 32792
  10.5 0.0 copy-start.8
  10.5 0.7 %copy-done.8 = s32[4,64]{1,0:T(4,128)S(1)} copy-done((s32[4,64]{1,0:T(4,128)S(1)}, s32[4,64]{1,0:T(4,128)}, u32[]{:S(2)}) %copy-start.8) | copy-done | bytes 1048
  11.2 20.6 %shard_map.113 = (f32[4,32]{1,0:T(4,128)S(1)}, f32[4,64]{1,0:T(4,128)S(1)}) custom-call(s32[1]{0:T(128)S(6)} %copy.14.lengths, bf16[2,1,128,4096]{3,2,1,0:T(8,128)(2,1)S(1)} %copy-done, bf16[2,1,128,4096]{3,2,1,0:T(8,128)(2,1)S(1)} %copy-done.1, bf16[2,64,4096]{2,1,0:T(8,128)(2,1)S(1)} %bitcast.3, bf16[2,64,4096]{2,1,0:T(8,128)(2,1)S(1)} %bitcast.4, ...), custom_call_target="tpu_custom_call" | custom-call | tf_op jit(solution)/shard_map/pallas_call | solution.py:207
  31.8 0.6 %copy.15 = f32[32,4]{0,1:T(4,128)} copy(f32[32,4]{0,1:T(4,128)S(1)} %bitcast.5) | data formatting | bytes 1024
  32.3 0.6 %copy.16 = f32[4,64]{1,0:T(4,128)} copy(f32[4,64]{1,0:T(4,128)S(1)} %get-tuple-element.9) | data formatting | bytes 2048
Async XLA Ops:
  1.3 1.6 %copy-start = (bf16[2,1,128,4096]{3,2,1,0:T(8,128)(2,1)S(1)}, bf16[2,1,128,4096]{3,2,1,0:T(8,128)(2,1)}, u32[]{:S(2)}) copy-start(bf16[2,1,128,4096]{3,2,1,0:T(8,128)(2,1)} %acts_hbm.1) | copy-start | bytes 6291460
  2.9 1.6 %copy-start.1 = (bf16[2,1,128,4096]{3,2,1,0:T(8,128)(2,1)S(1)}, bf16[2,1,128,4096]{3,2,1,0:T(8,128)(2,1)}, u32[]{:S(2)}) copy-start(bf16[2,1,128,4096]{3,2,1,0:T(8,128)(2,1)} %grads_hbm.1) | copy-start | bytes 6291460
  4.5 1.2 %copy-start.2 = (bf16[2,4096,64]{1,2,0:T(8,128)(2,1)S(1)}, bf16[2,4096,64]{1,2,0:T(8,128)(2,1)}, u32[]{:S(2)}) copy-start(bf16[2,4096,64]{1,2,0:T(8,128)(2,1)} %param.13) | copy-start | bytes 3145732
  5.7 1.2 %copy-start.3 = (bf16[2,4096,64]{1,2,0:T(8,128)(2,1)S(1)}, bf16[2,4096,64]{1,2,0:T(8,128)(2,1)}, u32[]{:S(2)}) copy-start(bf16[2,4096,64]{1,2,0:T(8,128)(2,1)} %param.14) | copy-start | bytes 3145732
  6.9 1.0 %copy-start.4 = (bf16[32,8192]{1,0:T(8,128)(2,1)S(1)}, bf16[32,8192]{1,0:T(8,128)(2,1)}, u32[]{:S(2)}) copy-start(bf16[32,8192]{1,0:T(8,128)(2,1)} %store_hbm.1) | copy-start | bytes 1572868
  8.0 0.8 %copy-start.5 = (f32[2,64,64]{2,1,0:T(8,128)S(1)}, f32[2,64,64]{2,1,0:T(8,128)}, u32[]{:S(2)}) copy-start(f32[2,64,64]{2,1,0:T(8,128)} %bin_hbm.1) | copy-start | bytes 98308
  8.8 0.8 %copy-start.6 = (f32[2,64,64]{2,1,0:T(8,128)S(1)}, f32[2,64,64]{2,1,0:T(8,128)}, u32[]{:S(2)}) copy-start(f32[2,64,64]{2,1,0:T(8,128)} %bout_hbm.1) | copy-start | bytes 98308
  9.6 0.8 %copy-start.7 = (f32[2,64,64]{2,1,0:T(8,128)S(1)}, f32[2,64,64]{2,1,0:T(8,128)}, u32[]{:S(2)}) copy-start(f32[2,64,64]{2,1,0:T(8,128)} %eig_hbm.1) | copy-start | bytes 98308
  10.5 0.7 %copy-start.8 = (s32[4,64]{1,0:T(4,128)S(1)}, s32[4,64]{1,0:T(4,128)}, u32[]{:S(2)}) copy-start(s32[4,64]{1,0:T(4,128)} %cand_hbm.1) | copy-start | bytes 3076

commit v2 on v1

--- a/solution.py
+++ b/solution.py
@@ -203,7 +203,7 @@
     n = nr * ns
     dma = pltpu.SemaphoreType.DMA
     vm = pltpu.VMEM
-    hbm = pl.BlockSpec(memory_space=pl.ANY)
+    hbm = pl.BlockSpec(memory_space=pltpu.HBM)
     scores, picked = pl.pallas_call(
         functools.partial(kernel, nr, ns),
         out_shape=(
@@ -226,7 +226,7 @@
             dma((n - 1,)), dma((n - 1,)),
         ],
         compiler_params=pltpu.CompilerParams(
-            collective_id=0, has_side_effects=True, vmem_limit_bytes=32 * 2**20),
+            collective_id=0, has_side_effects=True, vmem_limit_bytes=60 * 2**20),
     )(
         lengths, activations, out_grads,
         jnp.swapaxes(proj_in, 1, 2), jnp.swapaxes(proj_out, 1, 2),

time: 33.4 us -> 24.5 us (0.73)
  local copies, waits for them, and re-layouts: 11 us -> 2.48 us
    unnamed x20 -> x2, local copies, waits for them, and re-layouts: 11 us -> 2.48 us
where the time goes in v2:
time: 24.5 us; the launch traced here: 24.3 us
  Pallas kernels  20.5 us (84%)
  local copies, waits for them, and re-layouts  2.48 us (10%)
  between operations  1.29 us (5%)
    pallas_call x1, Pallas kernels, body(): pl.pallas_call(functools.partial(kernel, nr, ns), out_shape=(jax.ShapeDty...  20.5 us
    unnamed x2, local copies, waits for them, and re-layouts  2.48 us

profile of v2, /device:TPU:0, one launch (start us, length us, event | category | flops | bytes accessed | tf_op | source)
XLA Modules:
  0.0 24.3 jit_solution(17543707011797875726)
XLA Ops:
  1.3 20.5 %shard_map.113 = (f32[4,32]{1,0:T(4,128)}, f32[4,64]{1,0:T(4,128)}) custom-call(s32[1]{0:T(128)S(6)} %copy.14.lengths, bf16[2,1,128,4096]{3,2,1,0:T(8,128)(2,1)} %acts_hbm.1, bf16[2,1,128,4096]{3,2,1,0:T(8,128)(2,1)} %grads_hbm.1, bf16[2,64,4096]{2,1,0:T(8,128)(2,1)} %bitcast.3, bf16[2,64,4096]{2,1,0:T(8,128)(2,1)} %bitcast.4, f32[2,64,64]{2,1,0:T(8,128)} %bin_hbm.1, ...), custom_call_target="tpu_custom_call" | custom-call | tf_op jit(solution)/shard_map/pallas_call | solution.py:207
  21.8 1.2 %copy.15 = f32[32,4]{0,1:T(4,128)} copy(f32[32,4]{0,1:T(4,128)} %bitcast.5) | data formatting | bytes 1024
  23.1 1.2 %copy.16 = f32[4,64]{1,0:T(4,128)} copy(f32[4,64]{1,0:T(4,128)} %get-tuple-element.9) | data formatting | bytes 2048

commit v3 on v2

--- a/solution.py
+++ b/solution.py
@@ -82,8 +82,10 @@
         to = lax.rem(me + e + 1, n)
         return {"rows": to // ns, "seq": lax.rem(to, ns)}
 
-    each(n - 1, lambda e: pl.semaphore_signal(
-        barrier, inc=1, device_id=peer(e), device_id_type=MESH))
+    each(ns - 1, lambda d: pl.semaphore_signal(
+        barrier, inc=1, device_id={"seq": lax.rem(seq + d + 1, ns)}, device_id_type=MESH))
+    each(nr - 1, lambda d: pl.semaphore_signal(
+        barrier, inc=1, device_id={"rows": lax.rem(row + d + 1, nr)}, device_id_type=MESH))
 
     for c in small[:3]:
         c.wait()
@@ -107,6 +109,7 @@
             send_sem=gs_sem.at[l, d], recv_sem=gr_sem.at[l, d],
             device_id={"seq": lax.rem(seq + d + 1, ns)}, device_id_type=MESH)
 
+    low = lax.broadcasted_iota(jnp.int32, (half, 2 * rank), 1) < rank
     own = []
     for l in range(nl):
         loads[l][0].wait()
@@ -116,11 +119,12 @@
         loads[l][2].wait()
         loads[l][3].wait()
         pgt = mm(pout[l], grads[l], NT).astype(BF16)
-        g = mm(pgt, pa)
+        g = mm(pgt, jnp.concatenate([pa, pa], axis=1))
+        g = jnp.where(low, g[:half], g[half:])
         own.append(g)
         gsend[l] = g.astype(BF16)
         if l == 0:
-            pl.semaphore_wait(barrier, n - 1)
+            pl.semaphore_wait(barrier, ns + nr - 2)
         each(ns - 1, lambda d: gcopy(l, d).start())
 
     tests = []
@@ -129,13 +133,13 @@
         for d in range(ns - 1):
             gcopy(l, d).wait_recv()
             total = total + grecv[l, d].astype(F32)
+        total = jnp.concatenate([total[:, :rank], total[:, rank:]], axis=0)
         y = mm3(split(total), bi[l])
         rot = mm3(bot[l], split(y))
         pre = rot / (eig[l] + damping)
         x2 = mm3(split(pre), bi2[l], NT)
         z = mm3(beo[l], split(x2))
-        lane = lax.broadcasted_iota(jnp.int32, (half, 2 * rank), 1)
-        t = jnp.where(lane < rank, z[:half], z[half:]).astype(BF16)
+        t = jnp.where(low, z[:half], z[half:]).astype(BF16)
         tsend[pl.ds(l * half, half), :] = t
         tests.append(t)
 
@@ -176,22 +180,17 @@
     def pcopy(e):
         return pltpu.make_async_remote_copy(
             src_ref=psend, dst_ref=precv.at[e],
-            send_sem=ps_sem.at[e], recv_sem=pr_sem.at[e],
+            send_sem=ps_sem.at[0], recv_sem=pr_sem.at[0],
             device_id=peer(e), device_id_type=MESH)
 
     each(n - 1, lambda e: pcopy(e).start())
-    picked_ref[...] = psend[...]
-
     for l in range(nl):
         each(ns - 1, lambda d: gcopy(l, d).wait_send())
     each(nr - 1, lambda d: tcopy(d).wait_send())
 
-    def add(e):
-        pcopy(e).wait_recv()
-        picked_ref[...] += precv[e]
-
-    each(n - 1, add)
-    each(n - 1, lambda e: pcopy(e).wait_send())
+    pltpu.make_async_copy(precv, precv, pr_sem.at[0]).wait()
+    picked_ref[...] = psend[...] + jnp.sum(precv[...], axis=0)
+    pltpu.make_async_copy(precv, precv, ps_sem.at[0]).wait()
 
 
 def body(nr, ns, activations, out_grads, lengths, proj_in, proj_out,
@@ -206,10 +205,7 @@
     hbm = pl.BlockSpec(memory_space=pltpu.HBM)
     scores, picked = pl.pallas_call(
         functools.partial(kernel, nr, ns),
-        out_shape=(
-            jax.ShapeDtypeStruct((batch, rdev), F32),
-            jax.ShapeDtypeStruct((batch, topk), F32),
-        ),
+        out_shape=(pltpu.VMEM((batch, rdev), F32), pltpu.VMEM((batch, topk), F32)),
         in_specs=[pl.BlockSpec(memory_space=pltpu.SMEM)] + [hbm] * 9,
         out_specs=(pl.BlockSpec(memory_space=pltpu.VMEM),) * 2,
         scratch_shapes=[
@@ -217,13 +213,13 @@
             vm((nl, rank, width), BF16), vm((nl, rank, width), BF16),
             vm((nl, rank, rank), F32), vm((nl, rank, rank), F32), vm((nl, rank, rank), F32),
             vm((rdev, flat), BF16), vm((batch, topk), jnp.int32),
-            vm((nl, rank, rank), BF16), vm((nl, ns - 1, rank, rank), BF16),
+            vm((nl, rank // 2, 2 * rank), BF16), vm((nl, ns - 1, rank // 2, 2 * rank), BF16),
             vm((nl * rank // 2, 2 * rank), BF16), vm((nr - 1, nl * rank // 2, 2 * rank), BF16),
             vm((batch, topk), F32), vm((n - 1, batch, topk), F32),
             dma((nl, 4)), dma((5,)),
             dma((nl, ns - 1)), dma((nl, ns - 1)),
             dma((nr - 1,)), dma((nr - 1,)),
-            dma((n - 1,)), dma((n - 1,)),
+            dma((1,)), dma((1,)),
         ],
         compiler_params=pltpu.CompilerParams(
             collective_id=0, has_side_effects=True, vmem_limit_bytes=60 * 2**20),

time: 24.5 us -> 21.5 us (0.88)
  Pallas kernels: 20.5 us -> 18.9 us
  local copies, waits for them, and re-layouts: 2.48 us -> 1.16 us
    pallas_call x1, Pallas kernels: 20.5 us -> 18.9 us  [body(): pl.pallas_call(functools.partial(kernel, nr, ns), out_shape=(pltpu.VMEM((...]
    unnamed x2, local copies, waits for them, and re-layouts: 2.48 us -> 1.16 us
where the time goes in v3:
time: 21.5 us; the launch traced here: 21.3 us
  Pallas kernels  18.9 us (88%)
  between operations  1.29 us (6%)
  local copies, waits for them, and re-layouts  1.16 us (5%)
    pallas_call x1, Pallas kernels, body(): pl.pallas_call(functools.partial(kernel, nr, ns), out_shape=(pltpu.VMEM((...  18.9 us
    unnamed x2, local copies, waits for them, and re-layouts  1.16 us

profile of v3, /device:TPU:0, one launch (start us, length us, event | category | flops | bytes accessed | tf_op | source)
XLA Modules:
  0.0 21.3 jit_solution(2426778105001109107)
XLA Ops:
  1.3 18.9 %shard_map.113 = (f32[4,32]{1,0:T(4,128)S(1)}, f32[4,64]{1,0:T(4,128)S(1)}) custom-call(s32[1]{0:T(128)S(6)} %copy.16.lengths, bf16[2,1,128,4096]{3,2,1,0:T(8,128)(2,1)} %acts_hbm.1, bf16[2,1,128,4096]{3,2,1,0:T(8,128)(2,1)} %grads_hbm.1, bf16[2,64,4096]{2,1,0:T(8,128)(2,1)} %bitcast.4, bf16[2,64,4096]{2,1,0:T(8,128)(2,1)} %bitcast.5, f32[2,64,64]{2,1,0:T(8,128)} %bin_hbm.1, ...), custom_call_target="tpu_custom_call" | custom-call | tf_op jit(solution)/shard_map/pallas_call | solution.py:206
  20.1 0.6 %copy.14 = f32[32,4]{0,1:T(4,128)} copy(f32[32,4]{0,1:T(4,128)S(1)} %bitcast.3) | data formatting | bytes 1024
  20.7 0.6 %copy.15 = f32[4,64]{1,0:T(4,128)} copy(f32[4,64]{1,0:T(4,128)S(1)} %get-tuple-element.7) | data formatting | bytes 2048

commit v4 on v3

--- a/solution.py
+++ b/solution.py
@@ -127,7 +127,13 @@
             pl.semaphore_wait(barrier, ns + nr - 2)
         each(ns - 1, lambda d: gcopy(l, d).start())
 
-    tests = []
+    def tcopy(l, d):
+        part = pl.ds(l * half, half)
+        return pltpu.make_async_remote_copy(
+            src_ref=tsend.at[part], dst_ref=trecv.at[d, part],
+            send_sem=ts_sem.at[l, d], recv_sem=tr_sem.at[l, d],
+            device_id={"rows": lax.rem(row + d + 1, nr)}, device_id_type=MESH)
+
     for l in range(nl):
         total = own[l]
         for d in range(ns - 1):
@@ -141,41 +147,40 @@
         z = mm3(beo[l], split(x2))
         t = jnp.where(low, z[:half], z[half:]).astype(BF16)
         tsend[pl.ds(l * half, half), :] = t
-        tests.append(t)
-
-    def tcopy(d):
-        return pltpu.make_async_remote_copy(
-            src_ref=tsend, dst_ref=trecv.at[d],
-            send_sem=ts_sem.at[d], recv_sem=tr_sem.at[d],
-            device_id={"rows": lax.rem(row + d + 1, nr)}, device_id_type=MESH)
-
-    each(nr - 1, lambda d: tcopy(d).start())
+        each(nr - 1, lambda d: tcopy(l, d).start())
 
     for c in small[3:]:
         c.wait()
     lanes = 2 * rank
-    chunks = nl * half
     eye = lax.broadcasted_iota(jnp.int32, (rdev, rdev), 0) == lax.broadcasted_iota(
         jnp.int32, (rdev, rdev), 1)
     rows_k = me * rdev + lax.broadcasted_iota(jnp.int32, (rdev, cand.shape[1]), 0)
 
-    def score(t, b):
+    def partial(t, l):
+        t = t.astype(F32)
         acc = [jnp.zeros((rdev, lanes), F32) for _ in range(2)]
-        for c in range(chunks):
-            s = store[:, c * lanes:(c + 1) * lanes].astype(F32)
+        for c in range(half):
+            at = (l * half + c) * lanes
+            s = store[:, at:at + lanes].astype(F32)
             acc[c % 2] = acc[c % 2] + s * t[c:c + 1, :]
-        col = jnp.sum(acc[0] + acc[1], axis=1, keepdims=True)
-        scores_ref[pl.ds(b, 1), :] = jnp.sum(jnp.where(eye, col, 0.0), axis=0, keepdims=True)
-        hit = cand[pl.ds(b, 1), :] == rows_k
-        psend[pl.ds(b, 1), :] = jnp.sum(jnp.where(hit, col, 0.0), axis=0, keepdims=True)
-
-    score(tsend[...].astype(F32), row)
-
-    def other(d):
-        tcopy(d).wait_recv()
-        score(trecv[d].astype(F32), lax.rem(row + nr - d - 1, nr))
-
-    each(nr - 1, other)
+        return acc[0] + acc[1]
+
+    sums = [None] * nr
+    for l in range(nl):
+        part = pl.ds(l * half, half)
+        for p in range(nr):
+            if p > 0:
+                tcopy(l, p - 1).wait_recv()
+            a = partial(tsend[part, :] if p == 0 else trecv[p - 1, part, :], l)
+            sums[p] = a if l == 0 else sums[p] + a
+            if l == nl - 1:
+                b = lax.rem(row + nr - p, nr)
+                col = jnp.sum(sums[p], axis=1, keepdims=True)
+                scores_ref[pl.ds(b, 1), :] = jnp.sum(
+                    jnp.where(eye, col, 0.0), axis=0, keepdims=True)
+                hit = cand[pl.ds(b, 1), :] == rows_k
+                psend[pl.ds(b, 1), :] = jnp.sum(
+                    jnp.where(hit, col, 0.0), axis=0, keepdims=True)
 
     def pcopy(e):
         return pltpu.make_async_remote_copy(
@@ -186,7 +191,7 @@
     each(n - 1, lambda e: pcopy(e).start())
     for l in range(nl):
         each(ns - 1, lambda d: gcopy(l, d).wait_send())
-    each(nr - 1, lambda d: tcopy(d).wait_send())
+        each(nr - 1, lambda d: tcopy(l, d).wait_send())
 
     pltpu.make_async_copy(precv, precv, pr_sem.at[0]).wait()
     picked_ref[...] = psend[...] + jnp.sum(precv[...], axis=0)
@@ -218,7 +223,7 @@
             vm((batch, topk), F32), vm((n - 1, batch, topk), F32),
             dma((nl, 4)), dma((5,)),
             dma((nl, ns - 1)), dma((nl, ns - 1)),
-            dma((nr - 1,)), dma((nr - 1,)),
+            dma((nl, nr - 1)), dma((nl, nr - 1)),
             dma((1,)), dma((1,)),
         ],
         compiler_params=pltpu.CompilerParams(

time: 21.5 us -> 21.3 us (level)
  no operation moved by 1% of the time
where the time goes in v4:
time: 21.3 us; the launch traced here: 21.2 us
  Pallas kernels  18.7 us (88%)
  between operations  1.29 us (6%)
  local copies, waits for them, and re-layouts  1.16 us (5%)
    pallas_call x1, Pallas kernels, body(): pl.pallas_call(functools.partial(kernel, nr, ns), out_shape=(pltpu.VMEM((...  18.7 us
    unnamed x2, local copies, waits for them, and re-layouts  1.16 us

profile of v4, /device:TPU:0, one launch (start us, length us, event | category | flops | bytes accessed | tf_op | source)
XLA Modules:
  0.0 21.2 jit_solution(5815327317107705634)
XLA Ops:
  1.3 18.7 %shard_map.113 = (f32[4,32]{1,0:T(4,128)S(1)}, f32[4,64]{1,0:T(4,128)S(1)}) custom-call(s32[1]{0:T(128)S(6)} %copy.16.lengths, bf16[2,1,128,4096]{3,2,1,0:T(8,128)(2,1)} %acts_hbm.1, bf16[2,1,128,4096]{3,2,1,0:T(8,128)(2,1)} %grads_hbm.1, bf16[2,64,4096]{2,1,0:T(8,128)(2,1)} %bitcast.4, bf16[2,64,4096]{2,1,0:T(8,128)(2,1)} %bitcast.5, f32[2,64,64]{2,1,0:T(8,128)} %bin_hbm.1, ...), custom_call_target="tpu_custom_call" | custom-call | tf_op jit(solution)/shard_map/pallas_call | solution.py:211
  20.0 0.6 %copy.14 = f32[32,4]{0,1:T(4,128)} copy(f32[32,4]{0,1:T(4,128)S(1)} %bitcast.3) | data formatting | bytes 1024
  20.6 0.6 %copy.15 = f32[4,64]{1,0:T(4,128)} copy(f32[4,64]{1,0:T(4,128)S(1)} %get-tuple-element.7) | data formatting | bytes 2048

commit v5 on v4

--- a/solution.py
+++ b/solution.py
@@ -26,6 +26,14 @@
 
 def mm3(a, b, dims=NN):
     return mm(a[0], b[0], dims) + (mm(a[0], b[1], dims) + mm(a[1], b[0], dims))
+
+
+def project(weights, rows, l):
+    quarter = rows.shape[2] // 4
+    a, b, c, d = (
+        mm(weights[l, :, i * quarter:(i + 1) * quarter], rows[l, :, i * quarter:(i + 1) * quarter], NT)
+        for i in range(4))
+    return (a + b) + (c + d)
 
 
 def each(count, step):
@@ -69,6 +77,13 @@
             (bin_hbm, bin_), (bout_hbm, bout), (eig_hbm, eig), (cand_hbm, cand), (store_hbm, store),
         ))
     ]
+    barrier = pltpu.get_barrier_semaphore()
+
+    each(ns - 1, lambda d: pl.semaphore_signal(
+        barrier, inc=1, device_id={"seq": lax.rem(seq + d + 1, ns)}, device_id_type=MESH))
+    each(nr - 1, lambda d: pl.semaphore_signal(
+        barrier, inc=1, device_id={"rows": lax.rem(row + d + 1, nr)}, device_id_type=MESH))
+
     for c in small[:4]:
         c.start()
     for group in loads:
@@ -76,16 +91,9 @@
             c.start()
     small[4].start()
 
-    barrier = pltpu.get_barrier_semaphore()
-
     def peer(e):
         to = lax.rem(me + e + 1, n)
         return {"rows": to // ns, "seq": lax.rem(to, ns)}
-
-    each(ns - 1, lambda d: pl.semaphore_signal(
-        barrier, inc=1, device_id={"seq": lax.rem(seq + d + 1, ns)}, device_id_type=MESH))
-    each(nr - 1, lambda d: pl.semaphore_signal(
-        barrier, inc=1, device_id={"rows": lax.rem(row + d + 1, nr)}, device_id_type=MESH))
 
     for c in small[:3]:
         c.wait()
@@ -100,13 +108,13 @@
         bot.append(split(jnp.transpose(bout[l])))
         beo.append(tuple(mm(order, x).astype(BF16) for x in split(bout[l])))
 
-    pos = seq * tok + lax.broadcasted_iota(jnp.int32, (tok, rank), 0)
+    pos = seq * tok + lax.broadcasted_iota(jnp.int32, (rank, tok), 1)
     keep = pos < lengths[0]
 
     def gcopy(l, d):
         return pltpu.make_async_remote_copy(
             src_ref=gsend.at[l], dst_ref=grecv.at[l, d],
-            send_sem=gs_sem.at[l, d], recv_sem=gr_sem.at[l, d],
+            send_sem=gs_sem.at[l], recv_sem=gr_sem.at[l],
             device_id={"seq": lax.rem(seq + d + 1, ns)}, device_id_type=MESH)
 
     low = lax.broadcasted_iota(jnp.int32, (half, 2 * rank), 1) < rank
@@ -114,12 +122,11 @@
     for l in range(nl):
         loads[l][0].wait()
         loads[l][1].wait()
-        pa = mm(acts[l], pin[l], NT).astype(BF16)
-        pa = jnp.where(keep, pa.astype(F32), 0.0).astype(BF16)
+        pat = jnp.where(keep, project(pin, acts, l), 0.0).astype(BF16)
         loads[l][2].wait()
         loads[l][3].wait()
-        pgt = mm(pout[l], grads[l], NT).astype(BF16)
-        g = mm(pgt, jnp.concatenate([pa, pa], axis=1))
+        pgt = project(pout, grads, l).astype(BF16)
+        g = mm(pgt, jnp.concatenate([pat, pat], axis=0), NT)
         g = jnp.where(low, g[:half], g[half:])
         own.append(g)
         gsend[l] = g.astype(BF16)
@@ -136,9 +143,8 @@
 
     for l in range(nl):
         total = own[l]
-        for d in range(ns - 1):
-            gcopy(l, d).wait_recv()
-            total = total + grecv[l, d].astype(F32)
+        pltpu.make_async_copy(grecv.at[l], grecv.at[l], gr_sem.at[l]).wait()
+        total = total + jnp.sum(grecv[l].astype(F32), axis=0)
         total = jnp.concatenate([total[:, :rank], total[:, rank:]], axis=0)
         y = mm3(split(total), bi[l])
         rot = mm3(bot[l], split(y))
@@ -190,7 +196,7 @@
 
     each(n - 1, lambda e: pcopy(e).start())
     for l in range(nl):
-        each(ns - 1, lambda d: gcopy(l, d).wait_send())
+        pltpu.make_async_copy(grecv.at[l], grecv.at[l], gs_sem.at[l]).wait()
         each(nr - 1, lambda d: tcopy(l, d).wait_send())
 
     pltpu.make_async_copy(precv, precv, pr_sem.at[0]).wait()
@@ -222,7 +228,7 @@
             vm((nl * rank // 2, 2 * rank), BF16), vm((nr - 1, nl * rank // 2, 2 * rank), BF16),
             vm((batch, topk), F32), vm((n - 1, batch, topk), F32),
             dma((nl, 4)), dma((5,)),
-            dma((nl, ns - 1)), dma((nl, ns - 1)),
+            dma((nl,)), dma((nl,)),
             dma((nl, nr - 1)), dma((nl, nr - 1)),
             dma((1,)), dma((1,)),
         ],

time: 21.3 us -> 21.3 us (level)
  no operation moved by 1% of the time
where the time goes in v5:
time: 21.3 us; the launch traced here: 21.2 us
  Pallas kernels  18.7 us (88%)
  between operations  1.29 us (6%)
  local copies, waits for them, and re-layouts  1.16 us (5%)
    pallas_call x1, Pallas kernels, body(): pl.pallas_call(functools.partial(kernel, nr, ns), out_shape=(pltpu.VMEM((...  18.7 us
    unnamed x2, local copies, waits for them, and re-layouts  1.16 us

profile of v5, /device:TPU:0, one launch (start us, length us, event | category | flops | bytes accessed | tf_op | source)
XLA Modules:
  0.0 21.2 jit_solution(10716223205382589831)
XLA Ops:
  1.3 18.7 %shard_map.113 = (f32[4,32]{1,0:T(4,128)S(1)}, f32[4,64]{1,0:T(4,128)S(1)}) custom-call(s32[1]{0:T(128)S(6)} %copy.16.lengths, bf16[2,1,128,4096]{3,2,1,0:T(8,128)(2,1)} %acts_hbm.1, bf16[2,1,128,4096]{3,2,1,0:T(8,128)(2,1)} %grads_hbm.1, bf16[2,64,4096]{2,1,0:T(8,128)(2,1)} %bitcast.4, bf16[2,64,4096]{2,1,0:T(8,128)(2,1)} %bitcast.5, f32[2,64,64]{2,1,0:T(8,128)} %bin_hbm.1, ...), custom_call_target="tpu_custom_call" | custom-call | tf_op jit(solution)/shard_map/pallas_call | solution.py:217
  20.0 0.6 %copy.14 = f32[32,4]{0,1:T(4,128)} copy(f32[32,4]{0,1:T(4,128)S(1)} %bitcast.3) | data formatting | bytes 1024
  20.6 0.6 %copy.15 = f32[4,64]{1,0:T(4,128)} copy(f32[4,64]{1,0:T(4,128)S(1)} %get-tuple-element.7) | data formatting | bytes 2048
